TPU v7x, 32 devices: a whole 2x2x4 slice. The times are simulated.
32 devices in a mesh: fsdp: 8 (over y, x, core), win: 4 (over z).
Axes of the slice: x: 2, y: 2, z: 4, core: 2. Of those that a mesh axis runs over, the one named last changes fastest.
Arguments:
- tokens: bfloat16 [16384, 2048], P(('fsdp', 'win')), may hold values from -16 to 16
- block_map: int32 [8, 4], P('fsdp'), may hold values from 0 to 3, each once within a row
- shift: int32 [8], P('fsdp'), may hold values from 1 to 2047
- ln_gain: float32 [2048], replicated, may hold values from 0.5 to 1.5
- w_query: bfloat16 [2048, 1024], P('fsdp'), may hold values from -1 to 1
- w_key: bfloat16 [2048, 1024], P('fsdp'), may hold values from -1 to 1
- w_value: bfloat16 [2048, 1024], P('fsdp'), may hold values from -0.125 to 0.125
- w_out: bfloat16 [1024, 2048], P('fsdp'), may hold values from -0.1875 to 0.1875
- logit_scale: float32 [16], replicated, may hold values from 1 to 300
Outputs:
- mixed: bfloat16 [16384, 2048], P(('fsdp', 'win'))
All inputs are finite; a program needn't handle non-finite values.
Results may differ from a plain program's by a relative error of at most 0.008.
Values may be sent and summed in bfloat16 or wider, within the bound.
A program may use at most 128 MiB of HBM per device.

v0:
```python
import jax
import jax.numpy as jnp
from jax import lax
from jax.sharding import PartitionSpec as P


def layer_norm(resid, gain):
    center = jnp.mean(resid, axis=-1, keepdims=True)
    centred = resid - center
    spread = jnp.mean(centred * centred, axis=-1, keepdims=True)
    return (centred * lax.rsqrt(spread + 1e-05) * gain).astype(jnp.bfloat16)


def unit_heads(values, head_count):
    split = values.reshape(values.shape[0], head_count, -1)
    scale = lax.rsqrt(jnp.sum(split * split, axis=-1, keepdims=True) + 1e-06)
    return (split * scale).astype(jnp.bfloat16)


def block_length():
    return 512


def per_device(tokens, block_map, shift, ln_gain, w_query, w_key, w_value, w_out, logit_scale):
    tok_rows = tokens.shape[0]
    head_count = logit_scale.shape[0]
    inner = w_query.shape[1]
    head_size = inner // head_count
    groups = lax.axis_size("win")
    member = lax.axis_index("win")
    block_row = block_map[0]
    offset = shift[0]
    resid = tokens.astype(jnp.float32)
    normed = layer_norm(resid, ln_gain)
    group_ids = jnp.arange(groups, dtype=jnp.int32)

    def region_of(index):
        owner = index // tok_rows
        picked = owner[:, None] == group_ids[None, :]
        block = jnp.sum(jnp.where(picked, block_row[None, :], 0), axis=1)
        return block * tok_rows + index % tok_rows >= offset

    pieces = (
        lax.all_gather(w_query, "fsdp", axis=0, tiled=True),
        lax.all_gather(w_key, "fsdp", axis=0, tiled=True),
        lax.all_gather(w_value, "fsdp", axis=0, tiled=True),
    )
    columns = normed
    query, key_full, value = tuple(
        (jnp.dot(columns, piece, preferred_element_type=jnp.float32) for piece in pieces)
    )
    q_unit = unit_heads(query, head_count)
    k_flat = unit_heads(key_full, head_count).reshape(tok_rows, inner)
    value_half = value.astype(jnp.bfloat16)
    own_region = region_of(member * tok_rows + jnp.arange(tok_rows, dtype=jnp.int32))
    start_state = (
        jnp.full((head_count, tok_rows), -1e30, jnp.float32),
        jnp.zeros((head_count, tok_rows), jnp.float32),
        jnp.zeros((tok_rows, head_count, head_size), jnp.float32),
    )

    def attend_block(carry, packed):
        best, total, accum = carry
        keys, values, regions = packed
        allowed = (own_region[:, None] == regions[None, :])[None]
        score = (
            jnp.einsum("ihd,jhd->hij", q_unit, keys, preferred_element_type=jnp.float32)
            * logit_scale[:, None, None]
        )
        score = jnp.where(allowed, score, -1e30)
        new_best = jnp.maximum(best, jnp.max(score, axis=-1))
        weight = jnp.where(allowed, jnp.exp(score - new_best[:, :, None]), 0.0)
        fade = jnp.exp(best - new_best)
        total = total * fade + jnp.sum(weight, axis=-1)
        accum = accum * fade.T[:, :, None] + jnp.einsum(
            "hij,jhd->ihd", weight.astype(jnp.bfloat16), values, preferred_element_type=jnp.float32
        )
        return ((new_best, total, accum), None)

    carry = start_state
    pieces = (
        lax.all_gather(k_flat, "win", axis=0, tiled=True),
        lax.all_gather(value_half, "win", axis=0, tiled=True),
    )
    count = pieces[0].shape[0]
    blk = block_length()
    nblk = count // blk
    keys = pieces[0].reshape(nblk, blk, head_count, head_size)
    values = pieces[1].reshape(nblk, blk, head_count, head_size)
    regions = region_of(jnp.arange(count, dtype=jnp.int32)).reshape(nblk, blk)
    carry, unused = lax.scan(attend_block, carry, (keys, values, regions))
    best, total, accum = carry
    attended = (accum / total.T[:, :, None]).reshape(tok_rows, inner).astype(jnp.bfloat16)
    columns = attended
    output_sum = jnp.dot(
        columns,
        lax.all_gather(w_out, "fsdp", axis=0, tiled=True),
        preferred_element_type=jnp.float32,
    )
    return (resid + output_sum).astype(jnp.bfloat16)


def solution(mesh):
    return jax.shard_map(
        per_device,
        mesh=mesh,
        in_specs=(
            P(("fsdp", "win"), None),
            P("fsdp", None),
            P("fsdp"),
            P(),
            P("fsdp", None),
            P("fsdp", None),
            P("fsdp", None),
            P("fsdp", None),
            P(),
        ),
        out_specs=P(("fsdp", "win"), None),
        check_vma=False,
    )
```

profile of v0, /device:TPU:0, one launch (start us, length us, event | category | flops | bytes accessed | tf_op | source)
XLA Modules:
  0.0 430.1 jit_solution(9494824374934924594)
XLA Ops:
  11.4 37.3 %all-gather.7.cloned.1.call-done = bf16[2048,1024]{1,0:T(8,128)(2,1)} async-done(((bf16[256,1024]{1,0:T(8,128)(2,1)}), bf16[2048,1024]{1,0:T(8,128)(2,1)}) %all-gather.7.cloned.1.call-update) | async-done | bytes 4194320 | tf_op jit(solution)/shard_map/all_gather | solution.py:45
  48.7 6.6 %fusion.41 = (f32[512,1024]{1,0:T(8,128)}, f32[512,1024]{1,0:T(8,128)}) fusion(bf16[2048,1024]{1,0:T(8,128)(2,1)} %all-gather.7.cloned.1.call-done, bf16[512,2048]{1,0:T(8,128)(2,1)S(1)} %copy-done.1, f32[2048]{0:T(1024)S(1)} %copy-done.4, f32[512]{0:T(512)S(1)} %add_rsqrt_fusion.2, f32[512]{0:T(512)S(1)} %broadcast_multiply_fusion.1), kind=kOutput, calls=%fused_computation.76 | convolution fusion | flops 2153250816 | bytes 10498048 | tf_op jit(solution)/shard_map/dot_general | solution.py:50
  68.4 18.9 %all-gather.13.cloned.1.call-done = bf16[2048,1024]{1,0:T(8,128)(2,1)} async-done(((bf16[256,1024]{1,0:T(8,128)(2,1)}), bf16[2048,1024]{1,0:T(8,128)(2,1)}) %all-gather.13.cloned.1.call-update) | async-done | bytes 4194320 | tf_op jit(solution)/shard_map/all_gather | solution.py:46
  87.3 5.6 %convolution_convert_fusion = bf16[512,1024]{1,0:T(8,128)(2,1)} fusion(bf16[2048,1024]{1,0:T(8,128)(2,1)} %all-gather.13.cloned.1.call-done, bf16[512,2048]{1,0:T(8,128)(2,1)S(1)} %copy-done.1, f32[2048]{0:T(1024)S(1)} %copy-done.4, f32[512]{0:T(512)S(1)} %add_rsqrt_fusion.2, f32[512]{0:T(512)S(1)} %broadcast_multiply_fusion.1), kind=kOutput, calls=%fused_computation.39 | convolution fusion | flops 2153250816 | bytes 7352320 | tf_op jit(solution)/shard_map/dot_general | solution.py:50
  94.5 31.4 %all-gather.11.cloned.1.call-done = bf16[2048,1024]{1,0:T(8,128)(2,1)} async-done(((bf16[256,1024]{1,0:T(8,128)(2,1)}), bf16[2048,1024]{1,0:T(8,128)(2,1)}) %all-gather.11.cloned.1.call-update) | async-done | bytes 4194320 | tf_op jit(solution)/shard_map/all_gather | solution.py:44
  126.0 4.7 %multiply_reduce_fusion = (f32[512,16]{0,1:T(8,128)S(1)}, f32[512,1024]{0,1:T(8,128)S(1)}) fusion(bf16[2048,1024]{1,0:T(8,128)(2,1)} %all-gather.11.cloned.1.call-done, bf16[512,2048]{1,0:T(8,128)(2,1)S(1)} %copy-done.1, f32[2048]{0:T(1024)S(1)} %copy-done.4, f32[512]{0:T(512)S(1)} %add_rsqrt_fusion.2, f32[512]{0:T(512)S(1)} %broadcast_multiply_fusion.1), kind=kOutput, calls=%fused_computation.37 | convolution fusion | flops 2153766912 | bytes 8433664 | tf_op jit(solution)/shard_map/dot_general | solution.py:50
  131.1 77.1 %all-gather.9.cloned.1.call-done = bf16[2048,1024]{1,0:T(8,128)(2,1)} async-done(((bf16[512,1024]{1,0:T(8,128)(2,1)}), bf16[2048,1024]{1,0:T(8,128)(2,1)}) %all-gather.9.cloned.1.call-update) | async-done | bytes 4194320 | tf_op jit(solution)/shard_map/all_gather | solution.py:82
  208.2 11.8 %reshape.112 = bf16[4,512,16,64]{3,2,1,0:T(8,128)(2,1)} reshape(bf16[2048,1024]{1,0:T(8,128)(2,1)} %all-gather.9.cloned.1.call-done) | data formatting | bytes 8388608 | tf_op jit(solution)/shard_map/reshape | solution.py:88
  220.0 9.8 %copy.29 = bf16[4,512,16,64]{1,3,2,0:T(8,128)(2,1)} copy(bf16[4,512,16,64]{3,2,1,0:T(8,128)(2,1)} %reshape.112) | data formatting | bytes 8388608
  229.8 59.2 %all-gather.15.cloned.1.call-done = bf16[2048,1024]{1,0:T(8,128)(2,1)} async-done(((bf16[512,1024]{1,0:T(8,128)(2,1)}), bf16[2048,1024]{1,0:T(8,128)(2,1)}) %all-gather.15.cloned.1.call-update) | async-done | bytes 4194320 | tf_op jit(solution)/shard_map/all_gather | solution.py:83
  288.9 11.7 %reshape.113 = bf16[4,512,16,64]{3,2,1,0:T(8,128)(2,1)} reshape(bf16[2048,1024]{1,0:T(8,128)(2,1)} %all-gather.15.cloned.1.call-done) | data formatting | bytes 8388608 | tf_op jit(solution)/shard_map/reshape | solution.py:89
  300.6 9.8 %copy.30 = bf16[4,512,16,64]{1,3,2,0:T(8,128)(2,1)} copy(bf16[4,512,16,64]{3,2,1,0:T(8,128)(2,1)} %reshape.113) | data formatting | bytes 8388608
  310.4 105.1 %while.15 = (s32[]{:T(128)}, f32[16,512]{1,0:T(8,128)S(1)}, f32[16,512]{1,0:T(8,128)S(1)}, f32[512,16,64]{0,2,1:T(8,128)}, pred[512]{0:T(512)(128)(4,1)S(1)}, /*...) while((s32[]{:T(128)}, f32[16,512]{1,0:T(8,128)S(1)}, ...), condition=%wide.region_9.10_spmd.clone, body=%wide.region_6.9_spmd.clone.sunk | while | flops 1130151936 | bytes 126356832 | solution.py:91
  310.6 9.1 %fusion.58 = (f32[16,512]{1,0:T(8,128)S(1)}, f32[16,512,512]{2,1,0:T(8,128)}) fusion(f32[16]{0:T(128)S(1)} %get-tuple-element.252, pred[512,512]{0,1:T(8,128)(4,1)S(1)} %broadcast_compare_fusion.2, bf16[512,16,64]{0,2,1:T(8,128)(2,1)S(1)} %get-tuple-element.251, bf16[4,512,16,64]{1,3,2,0:T(8,128)(2,1)} %get-tuple-element.250, s32[]{:T(128)} %get-tuple-element.232), kind=kOutput, calls=%fused_computation.2.clone.1 | convolution fusion | flops 549445632 | bytes 19169856 | tf_op jit(solution)/shard_map/while/body/eval_jaxpr/ihd,jhd->hij/dot_general | solution.py:67
  319.7 12.5 %bitcast_add_fusion.2 = f32[512,16,64]{0,2,1:T(8,128)} fusion(f32[512,16,64]{0,2,1:T(8,128)} %get-tuple-element.235, f32[16,512,512]{2,1,0:T(8,128)} %get-tuple-element.218, f32[16,512]{1,0:T(8,128)S(1)} %get-tuple-element.245, f32[16]{0:T(128)S(1)} %get-tuple-element.252, pred[512,512]{0,1:T(8,128)(4,1)S(1)} %broadcast_compare_fusion.2, ...), kind=kOutput, calls=%fused_computation.7.clone.1 | convolution fusion | flops 559415296 | bytes 22348352 | tf_op jit(solution)/shard_map/while/body/eval_jaxpr/hij,jhd->ihd/dot_general | solution.py:75
  332.2 4.2 fusion.60
  336.7 8.8 %fusion.58 = (f32[16,512]{1,0:T(8,128)S(1)}, f32[16,512,512]{2,1,0:T(8,128)}) fusion(f32[16]{0:T(128)S(1)} %get-tuple-element.252, pred[512,512]{0,1:T(8,128)(4,1)S(1)} %broadcast_compare_fusion.2, bf16[512,16,64]{0,2,1:T(8,128)(2,1)S(1)} %get-tuple-element.251, bf16[4,512,16,64]{1,3,2,0:T(8,128)(2,1)} %get-tuple-element.250, s32[]{:T(128)} %get-tuple-element.232), kind=kOutput, calls=%fused_computation.2.clone.1 | convolution fusion | flops 549445632 | bytes 19169856 | tf_op jit(solution)/shard_map/while/body/eval_jaxpr/ihd,jhd->hij/dot_general | solution.py:67
  345.6 12.9 %bitcast_add_fusion.2 = f32[512,16,64]{0,2,1:T(8,128)} fusion(f32[512,16,64]{0,2,1:T(8,128)} %get-tuple-element.235, f32[16,512,512]{2,1,0:T(8,128)} %get-tuple-element.218, f32[16,512]{1,0:T(8,128)S(1)} %get-tuple-element.245, f32[16]{0:T(128)S(1)} %get-tuple-element.252, pred[512,512]{0,1:T(8,128)(4,1)S(1)} %broadcast_compare_fusion.2, ...), kind=kOutput, calls=%fused_computation.7.clone.1 | convolution fusion | flops 559415296 | bytes 22348352 | tf_op jit(solution)/shard_map/while/body/eval_jaxpr/hij,jhd->ihd/dot_general | solution.py:75
  358.4 4.2 fusion.60
  363.0 8.8 %fusion.58 = (f32[16,512]{1,0:T(8,128)S(1)}, f32[16,512,512]{2,1,0:T(8,128)}) fusion(f32[16]{0:T(128)S(1)} %get-tuple-element.252, pred[512,512]{0,1:T(8,128)(4,1)S(1)} %broadcast_compare_fusion.2, bf16[512,16,64]{0,2,1:T(8,128)(2,1)S(1)} %get-tuple-element.251, bf16[4,512,16,64]{1,3,2,0:T(8,128)(2,1)} %get-tuple-element.250, s32[]{:T(128)} %get-tuple-element.232), kind=kOutput, calls=%fused_computation.2.clone.1 | convolution fusion | flops 549445632 | bytes 19169856 | tf_op jit(solution)/shard_map/while/body/eval_jaxpr/ihd,jhd->hij/dot_general | solution.py:67
  371.8 12.9 %bitcast_add_fusion.2 = f32[512,16,64]{0,2,1:T(8,128)} fusion(f32[512,16,64]{0,2,1:T(8,128)} %get-tuple-element.235, f32[16,512,512]{2,1,0:T(8,128)} %get-tuple-element.218, f32[16,512]{1,0:T(8,128)S(1)} %get-tuple-element.245, f32[16]{0:T(128)S(1)} %get-tuple-element.252, pred[512,512]{0,1:T(8,128)(4,1)S(1)} %broadcast_compare_fusion.2, ...), kind=kOutput, calls=%fused_computation.7.clone.1 | convolution fusion | flops 559415296 | bytes 22348352 | tf_op jit(solution)/shard_map/while/body/eval_jaxpr/hij,jhd->ihd/dot_general | solution.py:75
  389.2 8.8 %fusion.58 = (f32[16,512]{1,0:T(8,128)S(1)}, f32[16,512,512]{2,1,0:T(8,128)}) fusion(f32[16]{0:T(128)S(1)} %get-tuple-element.252, pred[512,512]{0,1:T(8,128)(4,1)S(1)} %broadcast_compare_fusion.2, bf16[512,16,64]{0,2,1:T(8,128)(2,1)S(1)} %get-tuple-element.251, bf16[4,512,16,64]{1,3,2,0:T(8,128)(2,1)} %get-tuple-element.250, s32[]{:T(128)} %get-tuple-element.232), kind=kOutput, calls=%fused_computation.2.clone.1 | convolution fusion | flops 549445632 | bytes 19169856 | tf_op jit(solution)/shard_map/while/body/eval_jaxpr/ihd,jhd->hij/dot_general | solution.py:67
  398.1 12.9 %bitcast_add_fusion.2 = f32[512,16,64]{0,2,1:T(8,128)} fusion(f32[512,16,64]{0,2,1:T(8,128)} %get-tuple-element.235, f32[16,512,512]{2,1,0:T(8,128)} %get-tuple-element.218, f32[16,512]{1,0:T(8,128)S(1)} %get-tuple-element.245, f32[16]{0:T(128)S(1)} %get-tuple-element.252, pred[512,512]{0,1:T(8,128)(4,1)S(1)} %broadcast_compare_fusion.2, ...), kind=kOutput, calls=%fused_computation.7.clone.1 | convolution fusion | flops 559415296 | bytes 22348352 | tf_op jit(solution)/shard_map/while/body/eval_jaxpr/hij,jhd->ihd/dot_general | solution.py:75
  417.3 5.9 %fusion.24 = bf16[512,2048]{1,0:T(8,128)(2,1)} fusion(bf16[512,2048]{1,0:T(8,128)(2,1)S(1)} %copy-done.1, bf16[512,1024]{0,1:T(8,128)(2,1)S(1)} %bitcast.60, bf16[1024,2048]{1,0:T(8,128)(2,1)} %all-gather.17.cloned.1.call-done), kind=kOutput, calls=%fused_computation.33 | convolution fusion | flops 2150629376 | bytes 9437184 | tf_op jit(solution)/shard_map/dot_general | solution.py:95
  (75 shorter events, 30.5 us)
Async XLA Ops:
  6.5 4.2 copy-start.1
  6.5 42.2 %copy-start.4 = (f32[2048]{0:T(1024)S(1)}, f32[2048]{0:T(1024)}, u32[]{:S(2)}) copy-start(f32[2048]{0:T(1024)} %param.14) | copy-start | bytes 24580
  6.5 42.2 %all-gather.7.cloned.1.call-start = ((), (), s32[]{:S(2)}) async-start(), calls=%async_computation | async-start | bytes 4718592 | tf_op jit(solution)/shard_map/all_gather | solution.py:45
  7.3 80.1 %all-gather.13.cloned.1.call-start = ((), (), s32[]{:S(2)}) async-start(), calls=%async_computation.3 | async-start | bytes 4718592 | tf_op jit(solution)/shard_map/all_gather | solution.py:46
  8.0 118.0 %all-gather.11.cloned.1.call-start = ((), (), s32[]{:S(2)}) async-start(), calls=%async_computation.2 | async-start | bytes 4718592 | tf_op jit(solution)/shard_map/all_gather | solution.py:44
  8.7 199.5 %all-gather.9.cloned.1.call-start = ((), (), s32[]{:S(2)}) async-start(), calls=%async_computation.1 | async-start | bytes 5242880 | tf_op jit(solution)/shard_map/all_gather | solution.py:82
  68.3 25.9 %copy-start.3 = (s32[1,4]{1,0:T(1,128)S(1)}, s32[1,4]{1,0:T(1,128)}, u32[]{:S(2)}) copy-start(s32[1,4]{1,0:T(1,128)} %param.12) | copy-start | bytes 52
  68.4 220.6 %all-gather.15.cloned.1.call-start = ((), (), s32[]{:S(2)}) async-start(), calls=%async_computation.4 | async-start | bytes 5242880 | tf_op jit(solution)/shard_map/all_gather | solution.py:83
  93.0 324.4 %all-gather.17.cloned.1.call-start = ((), (), s32[]{:S(2)}) async-start(), calls=%async_computation.5 | async-start | bytes 4718592 | tf_op jit(solution)/shard_map/all_gather | solution.py:97
  300.6 9.8 %copy-start.2 = (f32[16]{0:T(128)S(1)}, f32[16]{0:T(128)}, u32[]{:S(2)}) copy-start(f32[16]{0:T(128)} %param.19) | copy-start | bytes 196
  319.7 12.5 %copy-start = (f32[16,512,512]{2,1,0:T(8,128)S(1)}, f32[16,512,512]{2,1,0:T(8,128)}, u32[]{:S(2)}) copy-start(f32[16,512,512]{2,1,0:T(8,128)} %get-tuple-element.218) | copy-start | bytes 50331652 | tf_op jit(solution)/shard_map/while
  345.6 12.9 %copy-start = (f32[16,512,512]{2,1,0:T(8,128)S(1)}, f32[16,512,512]{2,1,0:T(8,128)}, u32[]{:S(2)}) copy-start(f32[16,512,512]{2,1,0:T(8,128)} %get-tuple-element.218) | copy-start | bytes 50331652 | tf_op jit(solution)/shard_map/while
  371.8 12.9 %copy-start = (f32[16,512,512]{2,1,0:T(8,128)S(1)}, f32[16,512,512]{2,1,0:T(8,128)}, u32[]{:S(2)}) copy-start(f32[16,512,512]{2,1,0:T(8,128)} %get-tuple-element.218) | copy-start | bytes 50331652 | tf_op jit(solution)/shard_map/while
  398.1 12.9 %copy-start = (f32[16,512,512]{2,1,0:T(8,128)S(1)}, f32[16,512,512]{2,1,0:T(8,128)}, u32[]{:S(2)}) copy-start(f32[16,512,512]{2,1,0:T(8,128)} %get-tuple-element.218) | copy-start | bytes 50331652 | tf_op jit(solution)/shard_map/while
Sparse Core Ops, SparseCore 0:
  9.2 39.4 all-gather.6
  50.6 36.7 all-gather.12
  89.2 36.7 all-gather.10
  127.4 80.7 all-gather.8
  209.6 79.2 all-gather.14
  290.7 35.2 all-gather.16
where the time goes:
time: 432 us; the launch traced here: 430 us
  waiting for transfers between devices  227 us (53%)
  matrix products  109 us (25%)
  local copies, waits for them, and re-layouts  50.6 us (12%)
  other arithmetic  28.5 us (7%)
  between operations  14.3 us (3%)
    all_gather x1, waiting for transfers between devices, per_device(): lax.all_gather(k_flat, 'win', axis=0, tiled=True)  77.1 us
    all_gather x1, waiting for transfers between devices, per_device(): lax.all_gather(value_half, 'win', axis=0, tiled=True)  59.2 us
    dot_general x4, matrix products, attend_block(): jnp.einsum('hij,jhd->ihd', weight.astype(jnp.bfloat16), values, preferred...  51.1 us
    all_gather x1, waiting for transfers between devices, per_device(): lax.all_gather(w_key, 'fsdp', axis=0, tiled=True)  37.3 us
    dot_general x4, matrix products, attend_block(): jnp.einsum('ihd,jhd->hij', q_unit, keys, preferred_element_type=jnp.float32)  35.6 us
    all_gather x1, waiting for transfers between devices, per_device(): lax.all_gather(w_query, 'fsdp', axis=0, tiled=True)  31.4 us
    unnamed x10, local copies, waits for them, and re-layouts  19.5 us
    all_gather x1, waiting for transfers between devices, per_device(): lax.all_gather(w_value, 'fsdp', axis=0, tiled=True)  18.9 us
  transfers between devices with their start and end apart: 6, of which 5 were waited for; matrix products, arithmetic and copies ran while one was open for 42% of the time, Pallas kernels for 0%

commit v1 on v0

--- a/solution.py
+++ b/solution.py
@@ -2,6 +2,27 @@
 import jax.numpy as jnp
 from jax import lax
 from jax.sharding import PartitionSpec as P
+
+
+def gather_around(array, axis, dim):
+    length, index, extent = (lax.axis_size(axis), lax.axis_index(axis), array.shape[dim])
+    right = [(i, (i + 1) % length) for i in range(length)]
+    left = [(i, (i - 1) % length) for i in range(length)]
+    out = jnp.zeros((*array.shape[:dim], length * extent, *array.shape[dim + 1 :]), array.dtype)
+    out = lax.dynamic_update_slice_in_dim(out, array, index * extent, axis=dim)
+    from_left = from_right = array
+    middle = length // 2
+    for step in range(1, middle + 1):
+        from_left = lax.ppermute(from_left, axis, right)
+        out = lax.dynamic_update_slice_in_dim(
+            out, from_left, (index - step) % length * extent, axis=dim
+        )
+        if step < length - middle:
+            from_right = lax.ppermute(from_right, axis, left)
+            out = lax.dynamic_update_slice_in_dim(
+                out, from_right, (index + step) % length * extent, axis=dim
+            )
+    return out
 
 
 def layer_norm(resid, gain):
@@ -80,7 +101,7 @@
     carry = start_state
     pieces = (
         lax.all_gather(k_flat, "win", axis=0, tiled=True),
-        lax.all_gather(value_half, "win", axis=0, tiled=True),
+        gather_around(value_half, "win", 0),
     )
     count = pieces[0].shape[0]
     blk = block_length()

time: 432 us -> 375 us (0.87)
  waiting for transfers between devices: 227 us -> 157 us
  local copies, waits for them, and re-layouts: 50.6 us -> 60 us
    ppermute x0 -> x3, waiting for transfers between devices: none -> 68.4 us  [the longest x2 52.6 us: gather_around(): from_left = lax.ppermute(from_left, axis, right)]
    all_gather x1 -> x0, waiting for transfers between devices: 59.2 us -> none  [per_device(): lax.all_gather(value_half, 'win', axis=0, tiled=True)]
    all_gather x1, waiting for transfers between devices: 77.1 us -> 24.8 us  [per_device(): lax.all_gather(k_flat, 'win', axis=0, tiled=True)]
    all_gather x1, waiting for transfers between devices: 31.4 us -> 4.92 us  [per_device(): lax.all_gather(w_query, 'fsdp', axis=0, tiled=True)]
    dynamic_update_slice x0 -> x4, local copies, waits for them, and re-layouts: none -> 7.13 us  [the longest x2 4.65 us: gather_around(): lax.dynamic_update_slice_in_dim(out, from_left, (index - step) % length *...]
    ppermute x0 -> x3, local copies, waits for them, and re-layouts: none -> 6.91 us  [the longest x2 4.64 us: gather_around(): from_left = lax.ppermute(from_left, axis, right)]
    unnamed x10 -> x14, local copies, waits for them, and re-layouts: 19.5 us -> 16.8 us
  transfers between devices with their start and end apart: 6 -> 8, of which waited for: 5 -> 7; matrix products, arithmetic and copies ran while one was open for 42% -> 51% of each run, Pallas kernels for 0% -> 0%
where the time goes in v1:
time: 375 us; the launch traced here: 374 us
  waiting for transfers between devices  157 us (42%)
  matrix products  111 us (30%)
  local copies, waits for them, and re-layouts  60 us (16%)
  other arithmetic  28.5 us (8%)
  between operations  14 us (4%)
  starting transfers between devices  4.04 us (1%)
    ppermute x2, waiting for transfers between devices, gather_around(): from_left = lax.ppermute(from_left, axis, right)  52.6 us
    dot_general x4, matrix products, attend_block(): jnp.einsum('hij,jhd->ihd', weight.astype(jnp.bfloat16), values, preferred...  51.1 us
    all_gather x1, waiting for transfers between devices, per_device(): lax.all_gather(w_key, 'fsdp', axis=0, tiled=True)  37.3 us
    dot_general x4, matrix products, attend_block(): jnp.einsum('ihd,jhd->hij', q_unit, keys, preferred_element_type=jnp.float32)  35.4 us
    all_gather x1, waiting for transfers between devices, per_device(): lax.all_gather(k_flat, 'win', axis=0, tiled=True)  24.8 us
    all_gather x1, waiting for transfers between devices, per_device(): lax.all_gather(w_value, 'fsdp', axis=0, tiled=True)  18.5 us
    dot_general x3, matrix products, per_device(): jnp.dot(columns, piece, preferred_element_type=jnp.float32)  18.2 us
    unnamed x14, local copies, waits for them, and re-layouts  16.8 us
  transfers between devices with their start and end apart: 8, of which 7 were waited for; matrix products, arithmetic and copies ran while one was open for 51% of the time, Pallas kernels for 0%

profile of v1, /device:TPU:0, one launch (start us, length us, event | category | flops | bytes accessed | tf_op | source)
XLA Modules:
  0.0 373.8 jit_solution(5075209497078917976)
XLA Ops:
  11.4 37.3 %all-gather.6.cloned.1.call-done = bf16[2048,1024]{1,0:T(8,128)(2,1)} async-done(((bf16[256,1024]{1,0:T(8,128)(2,1)}), bf16[2048,1024]{1,0:T(8,128)(2,1)}) %all-gather.6.cloned.1.call-update) | async-done | bytes 4194320 | tf_op jit(solution)/shard_map/all_gather | solution.py:66
  48.7 6.6 %fusion.41 = (f32[512,1024]{1,0:T(8,128)}, f32[512,1024]{1,0:T(8,128)}) fusion(bf16[2048,1024]{1,0:T(8,128)(2,1)} %all-gather.6.cloned.1.call-done, bf16[512,2048]{1,0:T(8,128)(2,1)S(1)} %copy-done.1, f32[2048]{0:T(1024)S(1)} %copy-done.6, f32[512]{0:T(512)S(1)} %add_rsqrt_fusion.2, f32[512]{0:T(512)S(1)} %broadcast_multiply_fusion.1), kind=kOutput, calls=%fused_computation.80 | convolution fusion | flops 2153250816 | bytes 10498048 | tf_op jit(solution)/shard_map/dot_general | solution.py:71
  68.9 18.5 %all-gather.12.cloned.1.call-done = bf16[2048,1024]{1,0:T(8,128)(2,1)} async-done(((bf16[256,1024]{1,0:T(8,128)(2,1)}), bf16[2048,1024]{1,0:T(8,128)(2,1)}) %all-gather.12.cloned.1.call-update) | async-done | bytes 4194320 | tf_op jit(solution)/shard_map/all_gather | solution.py:67
  87.3 5.6 %convolution_convert_fusion = bf16[512,1024]{1,0:T(8,128)(2,1)} fusion(bf16[2048,1024]{1,0:T(8,128)(2,1)} %all-gather.12.cloned.1.call-done, bf16[512,2048]{1,0:T(8,128)(2,1)S(1)} %copy-done.1, f32[2048]{0:T(1024)S(1)} %copy-done.6, f32[512]{0:T(512)S(1)} %add_rsqrt_fusion.2, f32[512]{0:T(512)S(1)} %broadcast_multiply_fusion.1), kind=kOutput, calls=%fused_computation.39 | convolution fusion | flops 2153250816 | bytes 7352320 | tf_op jit(solution)/shard_map/dot_general | solution.py:71
  97.7 23.3 %collective-permute-done = bf16[512,1024]{1,0:T(8,128)(2,1)} collective-permute-done((bf16[512,1024]{1,0:T(8,128)(2,1)}, bf16[512,1024]{1,0:T(8,128)(2,1)}, u32[]{:S(2)}, u32[]{:S(2)}) %collective-permute-start) | collective-permute-done | bytes 1048608 | tf_op jit(solution)/shard_map/ppermute | solution.py:16
  121.1 4.9 %all-gather.10.cloned.1.call-done = bf16[2048,1024]{1,0:T(8,128)(2,1)} async-done(((bf16[256,1024]{1,0:T(8,128)(2,1)}), bf16[2048,1024]{1,0:T(8,128)(2,1)}) %all-gather.10.cloned.1.call-update) | async-done | bytes 4194320 | tf_op jit(solution)/shard_map/all_gather | solution.py:65
  126.0 6.1 %multiply_reduce_fusion = (f32[512,16]{0,1:T(8,128)S(1)}, f32[512,1024]{0,1:T(8,128)}) fusion(bf16[2048,1024]{1,0:T(8,128)(2,1)} %all-gather.10.cloned.1.call-done, bf16[512,2048]{1,0:T(8,128)(2,1)S(1)} %copy-done.1, f32[2048]{0:T(1024)S(1)} %copy-done.6, f32[512]{0:T(512)S(1)} %add_rsqrt_fusion.2, f32[512]{0:T(512)S(1)} %broadcast_multiply_fusion.1), kind=kOutput, calls=%fused_computation.37 | convolution fusion | flops 2153766912 | bytes 8433664 | tf_op jit(solution)/shard_map/dot_general | solution.py:71
  138.9 15.8 %collective-permute-done.1 = bf16[512,1024]{1,0:T(8,128)(2,1)} collective-permute-done((bf16[512,1024]{1,0:T(8,128)(2,1)}, bf16[512,1024]{1,0:T(8,128)(2,1)}, u32[]{:S(2)}, u32[]{:S(2)}) %collective-permute-start.1) | collective-permute-done | bytes 1048608 | tf_op jit(solution)/shard_map/ppermute | solution.py:21
  161.5 29.3 %collective-permute-done.2 = bf16[512,1024]{1,0:T(8,128)(2,1)} collective-permute-done((bf16[512,1024]{1,0:T(8,128)(2,1)}, bf16[512,1024]{1,0:T(8,128)(2,1)}, u32[]{:S(2)}, u32[]{:S(2)}) %collective-permute-start.2) | collective-permute-done | bytes 1048608 | tf_op jit(solution)/shard_map/ppermute | solution.py:16
  195.4 7.8 %reshape.111 = bf16[4,512,16,64]{1,0,3,2:T(4,128)(2,1)} reshape(bf16[2048,1024]{0,1:T(8,128)(2,1)} %constant_dynamic-update-slice_fusion.3) | data formatting | bytes 8388608 | tf_op jit(solution)/shard_map/reshape | solution.py:110
  203.3 5.2 %copy.35 = bf16[4,512,16,64]{1,3,2,0:T(8,128)(2,1)} copy(bf16[4,512,16,64]{1,0,3,2:T(4,128)(2,1)} %reshape.111) | data formatting | bytes 8388608
  208.4 24.8 %all-gather.8.cloned.1.call-done = bf16[2048,1024]{1,0:T(8,128)(2,1)} async-done(((bf16[512,1024]{1,0:T(8,128)(2,1)}), bf16[2048,1024]{1,0:T(8,128)(2,1)}) %all-gather.8.cloned.1.call-update) | async-done | bytes 4194320 | tf_op jit(solution)/shard_map/all_gather | solution.py:103
  233.2 11.7 %reshape.112 = bf16[4,512,16,64]{3,2,1,0:T(8,128)(2,1)} reshape(bf16[2048,1024]{1,0:T(8,128)(2,1)} %all-gather.8.cloned.1.call-done) | data formatting | bytes 8388608 | tf_op jit(solution)/shard_map/reshape | solution.py:109
  245.0 9.7 %copy.34 = bf16[4,512,16,64]{1,3,2,0:T(8,128)(2,1)} copy(bf16[4,512,16,64]{3,2,1,0:T(8,128)(2,1)} %reshape.112) | data formatting | bytes 8388608
  254.7 104.7 %while.15 = (s32[]{:T(128)}, f32[16,512]{1,0:T(8,128)S(1)}, f32[16,512]{1,0:T(8,128)S(1)}, f32[512,16,64]{0,2,1:T(8,128)}, pred[512]{0:T(512)(128)(4,1)S(1)}, /*...) while((s32[]{:T(128)}, f32[16,512]{1,0:T(8,128)S(1)}, ...), condition=%wide.region_9.10_spmd.clone, body=%wide.region_6.9_spmd.clone.sunk | while | flops 1130151936 | bytes 126356832 | solution.py:112
  255.0 9.0 %fusion.58 = (f32[16,512]{1,0:T(8,128)S(1)}, f32[16,512,512]{2,1,0:T(8,128)}) fusion(f32[16]{0:T(128)S(1)} %get-tuple-element.252, pred[512,512]{0,1:T(8,128)(4,1)S(1)} %broadcast_compare_fusion.2, bf16[512,16,64]{0,2,1:T(8,128)(2,1)S(1)} %get-tuple-element.251, bf16[4,512,16,64]{1,3,2,0:T(8,128)(2,1)} %get-tuple-element.250, s32[]{:T(128)} %get-tuple-element.232), kind=kOutput, calls=%fused_computation.2.clone.1 | convolution fusion | flops 549445632 | bytes 19169856 | tf_op jit(solution)/shard_map/while/body/eval_jaxpr/ihd,jhd->hij/dot_general | solution.py:88
  264.0 12.5 %bitcast_add_fusion.2 = f32[512,16,64]{0,2,1:T(8,128)} fusion(f32[512,16,64]{0,2,1:T(8,128)} %get-tuple-element.235, f32[16,512,512]{2,1,0:T(8,128)} %get-tuple-element.218, f32[16,512]{1,0:T(8,128)S(1)} %get-tuple-element.245, f32[16]{0:T(128)S(1)} %get-tuple-element.252, pred[512,512]{0,1:T(8,128)(4,1)S(1)} %broadcast_compare_fusion.2, ...), kind=kOutput, calls=%fused_computation.7.clone.1 | convolution fusion | flops 559415296 | bytes 22348352 | tf_op jit(solution)/shard_map/while/body/eval_jaxpr/hij,jhd->ihd/dot_general | solution.py:96
  281.0 8.8 %fusion.58 = (f32[16,512]{1,0:T(8,128)S(1)}, f32[16,512,512]{2,1,0:T(8,128)}) fusion(f32[16]{0:T(128)S(1)} %get-tuple-element.252, pred[512,512]{0,1:T(8,128)(4,1)S(1)} %broadcast_compare_fusion.2, bf16[512,16,64]{0,2,1:T(8,128)(2,1)S(1)} %get-tuple-element.251, bf16[4,512,16,64]{1,3,2,0:T(8,128)(2,1)} %get-tuple-element.250, s32[]{:T(128)} %get-tuple-element.232), kind=kOutput, calls=%fused_computation.2.clone.1 | convolution fusion | flops 549445632 | bytes 19169856 | tf_op jit(solution)/shard_map/while/body/eval_jaxpr/ihd,jhd->hij/dot_general | solution.py:88
  289.8 12.9 %bitcast_add_fusion.2 = f32[512,16,64]{0,2,1:T(8,128)} fusion(f32[512,16,64]{0,2,1:T(8,128)} %get-tuple-element.235, f32[16,512,512]{2,1,0:T(8,128)} %get-tuple-element.218, f32[16,512]{1,0:T(8,128)S(1)} %get-tuple-element.245, f32[16]{0:T(128)S(1)} %get-tuple-element.252, pred[512,512]{0,1:T(8,128)(4,1)S(1)} %broadcast_compare_fusion.2, ...), kind=kOutput, calls=%fused_computation.7.clone.1 | convolution fusion | flops 559415296 | bytes 22348352 | tf_op jit(solution)/shard_map/while/body/eval_jaxpr/hij,jhd->ihd/dot_general | solution.py:96
  307.2 8.8 %fusion.58 = (f32[16,512]{1,0:T(8,128)S(1)}, f32[16,512,512]{2,1,0:T(8,128)}) fusion(f32[16]{0:T(128)S(1)} %get-tuple-element.252, pred[512,512]{0,1:T(8,128)(4,1)S(1)} %broadcast_compare_fusion.2, bf16[512,16,64]{0,2,1:T(8,128)(2,1)S(1)} %get-tuple-element.251, bf16[4,512,16,64]{1,3,2,0:T(8,128)(2,1)} %get-tuple-element.250, s32[]{:T(128)} %get-tuple-element.232), kind=kOutput, calls=%fused_computation.2.clone.1 | convolution fusion | flops 549445632 | bytes 19169856 | tf_op jit(solution)/shard_map/while/body/eval_jaxpr/ihd,jhd->hij/dot_general | solution.py:88
  316.1 12.9 %bitcast_add_fusion.2 = f32[512,16,64]{0,2,1:T(8,128)} fusion(f32[512,16,64]{0,2,1:T(8,128)} %get-tuple-element.235, f32[16,512,512]{2,1,0:T(8,128)} %get-tuple-element.218, f32[16,512]{1,0:T(8,128)S(1)} %get-tuple-element.245, f32[16]{0:T(128)S(1)} %get-tuple-element.252, pred[512,512]{0,1:T(8,128)(4,1)S(1)} %broadcast_compare_fusion.2, ...), kind=kOutput, calls=%fused_computation.7.clone.1 | convolution fusion | flops 559415296 | bytes 22348352 | tf_op jit(solution)/shard_map/while/body/eval_jaxpr/hij,jhd->ihd/dot_general | solution.py:96
  333.5 8.8 %fusion.58 = (f32[16,512]{1,0:T(8,128)S(1)}, f32[16,512,512]{2,1,0:T(8,128)}) fusion(f32[16]{0:T(128)S(1)} %get-tuple-element.252, pred[512,512]{0,1:T(8,128)(4,1)S(1)} %broadcast_compare_fusion.2, bf16[512,16,64]{0,2,1:T(8,128)(2,1)S(1)} %get-tuple-element.251, bf16[4,512,16,64]{1,3,2,0:T(8,128)(2,1)} %get-tuple-element.250, s32[]{:T(128)} %get-tuple-element.232), kind=kOutput, calls=%fused_computation.2.clone.1 | convolution fusion | flops 549445632 | bytes 19169856 | tf_op jit(solution)/shard_map/while/body/eval_jaxpr/ihd,jhd->hij/dot_general | solution.py:88
  342.3 12.9 %bitcast_add_fusion.2 = f32[512,16,64]{0,2,1:T(8,128)} fusion(f32[512,16,64]{0,2,1:T(8,128)} %get-tuple-element.235, f32[16,512,512]{2,1,0:T(8,128)} %get-tuple-element.218, f32[16,512]{1,0:T(8,128)S(1)} %get-tuple-element.245, f32[16]{0:T(128)S(1)} %get-tuple-element.252, pred[512,512]{0,1:T(8,128)(4,1)S(1)} %broadcast_compare_fusion.2, ...), kind=kOutput, calls=%fused_computation.7.clone.1 | convolution fusion | flops 559415296 | bytes 22348352 | tf_op jit(solution)/shard_map/while/body/eval_jaxpr/hij,jhd->ihd/dot_general | solution.py:96
  361.4 5.9 %fusion.24 = bf16[512,2048]{1,0:T(8,128)(2,1)} fusion(bf16[512,2048]{1,0:T(8,128)(2,1)S(1)} %copy-done.1, bf16[512,1024]{0,1:T(8,128)(2,1)S(1)} %bitcast.62, bf16[1024,2048]{1,0:T(8,128)(2,1)} %all-gather.14.cloned.1.call-done), kind=kOutput, calls=%fused_computation.33 | convolution fusion | flops 2150629376 | bytes 9437184 | tf_op jit(solution)/shard_map/dot_general | solution.py:116
  (91 shorter events, 60.6 us)
Async XLA Ops:
  6.5 4.2 %copy-start.1 = (bf16[512,2048]{1,0:T(8,128)(2,1)S(1)}, bf16[512,2048]{1,0:T(8,128)(2,1)}, u32[]{:S(2)}) copy-start(bf16[512,2048]{1,0:T(8,128)(2,1)} %param.11) | copy-start | bytes 6291460
  6.5 42.2 %copy-start.6 = (f32[2048]{0:T(1024)S(1)}, f32[2048]{0:T(1024)}, u32[]{:S(2)}) copy-start(f32[2048]{0:T(1024)} %param.14) | copy-start | bytes 24580
  6.5 42.2 %all-gather.6.cloned.1.call-start = ((), (), s32[]{:S(2)}) async-start(), calls=%async_computation | async-start | bytes 4718592 | tf_op jit(solution)/shard_map/all_gather | solution.py:66
  7.3 80.1 %all-gather.12.cloned.1.call-start = ((), (), s32[]{:S(2)}) async-start(), calls=%async_computation.3 | async-start | bytes 4718592 | tf_op jit(solution)/shard_map/all_gather | solution.py:67
  8.0 118.0 %all-gather.10.cloned.1.call-start = ((), (), s32[]{:S(2)}) async-start(), calls=%async_computation.2 | async-start | bytes 4718592 | tf_op jit(solution)/shard_map/all_gather | solution.py:65
  8.7 224.5 %all-gather.8.cloned.1.call-start = ((), (), s32[]{:S(2)}) async-start(), calls=%async_computation.1 | async-start | bytes 5242880 | tf_op jit(solution)/shard_map/all_gather | solution.py:103
  68.3 293.1 %all-gather.14.cloned.1.call-start = ((), (), s32[]{:S(2)}) async-start(), calls=%async_computation.4 | async-start | bytes 4718592 | tf_op jit(solution)/shard_map/all_gather | solution.py:118
  68.8 26.2 %copy-start.5 = (s32[1,4]{1,0:T(1,128)S(1)}, s32[1,4]{1,0:T(1,128)}, u32[]{:S(2)}) copy-start(s32[1,4]{1,0:T(1,128)} %param.12) | copy-start | bytes 52
  92.9 28.1 %collective-permute-start = (bf16[512,1024]{1,0:T(8,128)(2,1)}, bf16[512,1024]{1,0:T(8,128)(2,1)}, u32[]{:S(2)}, u32[]{:S(2)}) collective-permute-start(bf16[512,1024]{1,0:T(8,128)(2,1)} %convolution_convert_fusion), channel_id=1, source_target_pairs={{0,1},{1,2},{2,3},{3,0},{4,5},{5,6},{6,7},{7,4},{8,9},{9,10},{10,1... | collective-permute-start | bytes 3145736 | tf_op jit(solution)/shard_map/ppermute | solution.py:16
  95.3 59.3 %collective-permute-start.1 = (bf16[512,1024]{1,0:T(8,128)(2,1)}, bf16[512,1024]{1,0:T(8,128)(2,1)}, u32[]{:S(2)}, u32[]{:S(2)}) collective-permute-start(bf16[512,1024]{1,0:T(8,128)(2,1)} %convolution_convert_fusion), channel_id=1, source_target_pairs={{0,3},{1,0},{2,1},{3,2},{4,7},{5,4},{6,5},{7,6},{8,11},{9,8},{10,9... | collective-permute-start | bytes 3145736 | tf_op jit(solution)/shard_map/ppermute | solution.py:21
  121.1 69.8 %collective-permute-start.2 = (bf16[512,1024]{1,0:T(8,128)(2,1)}, bf16[512,1024]{1,0:T(8,128)(2,1)}, u32[]{:S(2)}, u32[]{:S(2)}) collective-permute-start(bf16[512,1024]{1,0:T(8,128)(2,1)} %collective-permute-done), channel_id=1, source_target_pairs={{0,1},{1,2},{2,3},{3,0},{4,5},{5,6},{6,7},{7,4},{8,9},{9,10},{10,1... | collective-permute-start | bytes 3145736 | tf_op jit(solution)/shard_map/ppermute | solution.py:16
  133.5 2.7 copy-start.3
  134.2 1.9 copy-start.2
  245.0 9.8 %copy-start.4 = (f32[16]{0:T(128)S(1)}, f32[16]{0:T(128)}, u32[]{:S(2)}) copy-start(f32[16]{0:T(128)} %param.19) | copy-start | bytes 196
  264.0 12.5 %copy-start = (f32[16,512,512]{2,1,0:T(8,128)S(1)}, f32[16,512,512]{2,1,0:T(8,128)}, u32[]{:S(2)}) copy-start(f32[16,512,512]{2,1,0:T(8,128)} %get-tuple-element.218) | copy-start | bytes 50331652 | tf_op jit(solution)/shard_map/while
  289.8 12.9 %copy-start = (f32[16,512,512]{2,1,0:T(8,128)S(1)}, f32[16,512,512]{2,1,0:T(8,128)}, u32[]{:S(2)}) copy-start(f32[16,512,512]{2,1,0:T(8,128)} %get-tuple-element.218) | copy-start | bytes 50331652 | tf_op jit(solution)/shard_map/while
  316.0 12.9 %copy-start = (f32[16,512,512]{2,1,0:T(8,128)S(1)}, f32[16,512,512]{2,1,0:T(8,128)}, u32[]{:S(2)}) copy-start(f32[16,512,512]{2,1,0:T(8,128)} %get-tuple-element.218) | copy-start | bytes 50331652 | tf_op jit(solution)/shard_map/while
  342.3 12.9 %copy-start = (f32[16,512,512]{2,1,0:T(8,128)S(1)}, f32[16,512,512]{2,1,0:T(8,128)}, u32[]{:S(2)}) copy-start(f32[16,512,512]{2,1,0:T(8,128)} %get-tuple-element.218) | copy-start | bytes 50331652 | tf_op jit(solution)/shard_map/while
Sparse Core Ops, SparseCore 0:
  9.2 39.4 all-gather.5
  50.6 36.7 all-gather.11
  89.2 36.7 all-gather.9
  127.4 105.7 all-gather.7
  235.0 34.7 all-gather.13
